TPU v7x, 32 devices: a whole 2x2x4 slice. The times are simulated.
32 devices in a mesh: groups: 2 (over x), expert: 16 (over z, y, core).
Axes of the slice: x: 2, y: 2, z: 4, core: 2. Of those that a mesh axis runs over, the one named last changes fastest.
Arguments:
- tokens: bfloat16 [4096, 2048], P(('groups', 'expert')), parts along dimension 0, may hold values from -6 to 6
- out_grad: bfloat16 [4096, 2048], P(('groups', 'expert')), parts along dimension 0, may hold values from -6 to 6
- gate_probs: float32 [4096, 8], P(('groups', 'expert')), parts along dimension 0, may hold values from 0.05 to 0.2
- routes: int32 [4096, 8], P(('groups', 'expert')), parts along dimension 0, may hold values from 0 to 15, all different within a row; in each aligned block of 128 rows (0 to 127, 128 to 255, ...) at most 80 rows name the same one
- w_gate: bfloat16 [16, 2048, 384], P('expert'), may hold values from -0.125 to 0.125
- w_up: bfloat16 [16, 2048, 384], P('expert'), may hold values from -0.125 to 0.125
- w_down: bfloat16 [16, 384, 2048], P('expert'), may hold values from -0.3125 to 0.3125
Outputs:
- tokens_grad: bfloat16 [4096, 2048], P(('groups', 'expert')), parts along dimension 0
- gate_wgrad: bfloat16 [32, 2048, 384], P(('groups', 'expert')), parts along dimension 0
- up_wgrad: bfloat16 [32, 2048, 384], P(('groups', 'expert')), parts along dimension 0
- down_wgrad: bfloat16 [32, 384, 2048], P(('groups', 'expert')), parts along dimension 0
There are 2 independent parts, one for each index of `groups`. A program takes and returns all parts, laid end to end along the dimension named above; an argument that names none is the same for every part. Nothing has to cross between parts.
Inputs may be any that keep to these rules, and one draw needn't show every extreme that they name: A token's 8 experts differ. Among the 128 tokens of one block no expert is named by more than 80 routes, and in some block one expert is named by exactly 80.
All inputs are finite; a program needn't handle non-finite values.
Results may differ from a plain program's by a relative error of at most 0.0064.
Values may be sent and summed in bfloat16 or wider, within the bound.
No kernel may reach another device: no remote copies, remote signals or barrier semaphores. Data moves between devices by JAX's collectives and lax.ppermute only.
A program may use at most 128 MiB of HBM per device.

v0:
```python
import jax
import jax.numpy as jnp
from jax import lax
from jax.sharding import PartitionSpec as P


def expert_rows(inputs, grads_in, weight_gate, weight_up, weight_down):
    gate_pre = jnp.dot(inputs, weight_gate, preferred_element_type=jnp.float32)
    up_pre = jnp.dot(inputs, weight_up, preferred_element_type=jnp.float32)
    sigmoid_gate = jax.nn.sigmoid(gate_pre)
    activated = gate_pre * sigmoid_gate
    hidden = (activated * up_pre).astype(jnp.bfloat16)
    hidden_grad = jnp.dot(grads_in, weight_down.T, preferred_element_type=jnp.float32)
    up_grad = (hidden_grad * activated).astype(jnp.bfloat16)
    gate_grad = (
        hidden_grad * up_pre * sigmoid_gate * (1.0 + gate_pre * (1.0 - sigmoid_gate))
    ).astype(jnp.bfloat16)
    row_grad = (
        jnp.dot(gate_grad, weight_gate.T, preferred_element_type=jnp.float32)
        + jnp.dot(up_grad, weight_up.T, preferred_element_type=jnp.float32)
    ).astype(jnp.bfloat16)
    return (hidden, gate_grad, up_grad, row_grad)


def slot_numbers(expert_ids, experts):
    onehot = (expert_ids[:, None] == jnp.arange(experts, dtype=jnp.int32)[None, :]).astype(
        jnp.int32
    )
    running = jnp.cumsum(onehot, axis=0, dtype=jnp.int32)
    return (
        jnp.sum(running * onehot, axis=1, dtype=jnp.int32) - 1,
        jnp.sum(onehot, axis=0, dtype=jnp.int32),
    )


def local(tokens, out_grad, gate_probs, routes, w_gate, w_up, w_down):
    experts = lax.axis_size("expert")
    tok_count = tokens.shape[0]
    width = tokens.shape[1]
    top_count = routes.shape[1]
    capacity = tok_count * top_count * 5 // (4 * experts)
    row_total = experts * capacity
    weight_gate = w_gate[0]
    weight_up = w_up[0]
    weight_down = w_down[0]
    expert_ids = routes.reshape(-1)
    slots, counts = slot_numbers(expert_ids, experts)
    places = expert_ids * capacity + slots
    route_inputs = jnp.repeat(tokens, top_count, axis=0)
    route_grads = (
        (gate_probs[:, :, None] * out_grad[:, None, :].astype(jnp.float32))
        .astype(jnp.bfloat16)
        .reshape(-1, width)
    )
    send_inputs = (
        jnp.zeros((row_total, width), jnp.bfloat16)
        .at[places]
        .set(route_inputs)
        .reshape(experts, capacity, width)
    )
    send_grads = (
        jnp.zeros((row_total, width), jnp.bfloat16)
        .at[places]
        .set(route_grads)
        .reshape(experts, capacity, width)
    )
    got_inputs, got_grads = (
        lax.all_to_all(send_inputs, "expert", split_axis=0, concat_axis=0, tiled=True),
        lax.all_to_all(send_grads, "expert", split_axis=0, concat_axis=0, tiled=True),
    )
    flat_in = got_inputs.reshape(row_total, width)
    flat_grad = got_grads.reshape(row_total, width)
    hidden, gate_grad, up_grad, row_grad = expert_rows(
        flat_in, flat_grad, weight_gate, weight_up, weight_down
    )
    returned = lax.all_to_all(
        row_grad.reshape(experts, capacity, width),
        "expert",
        split_axis=0,
        concat_axis=0,
        tiled=True,
    )
    gate_acc = jnp.dot(flat_in.T, gate_grad, preferred_element_type=jnp.float32)
    up_acc = jnp.dot(flat_in.T, up_grad, preferred_element_type=jnp.float32)
    down_acc = jnp.dot(hidden.T, flat_grad, preferred_element_type=jnp.float32)
    gathered = returned.reshape(row_total, width)[places].reshape(tok_count, top_count, width)
    tokens_grad = jnp.sum(gathered, axis=1, dtype=jnp.float32).astype(jnp.bfloat16)
    gate_wgrad = gate_acc.astype(jnp.bfloat16)[None]
    up_wgrad = up_acc.astype(jnp.bfloat16)[None]
    down_wgrad = down_acc.astype(jnp.bfloat16)[None]
    return (tokens_grad, gate_wgrad, up_wgrad, down_wgrad)


def solution(mesh):
    return jax.shard_map(
        local,
        mesh=mesh,
        in_specs=(
            P(("groups", "expert"), None),
            P(("groups", "expert"), None),
            P(("groups", "expert"), None),
            P(("groups", "expert"), None),
            P("expert", None, None),
            P("expert", None, None),
            P("expert", None, None),
        ),
        out_specs=(
            P(("groups", "expert"), None),
            P(("groups", "expert"), None, None),
            P(("groups", "expert"), None, None),
            P(("groups", "expert"), None, None),
        ),
        check_vma=False,
    )
```

profile of v0, /device:TPU:13, one launch (start us, length us, event | category | flops | bytes accessed | tf_op | source)
XLA Modules:
  0.0 412.5 jit_solution(14100621843344244033)
XLA Ops:
  0.6 0.8 broadcast_multiply_fusion
  1.5 0.8 copy.14
  2.4 0.1 copy.13
  2.6 4.5 %reduce-window.6 = s32[16,8,128]{2,1,0:T(8,128)S(1)} reduce-window(s32[16,8,128]{2,1,0:T(8,128)S(1)} %fusion.26, s32[]{:T(128)} %constant.8.clone.1), window={size=1x1x128 pad=0_0x0_0x127_0}, to_apply=%region_0.0 | reduce-window | flops 2080768 | bytes 131076 | tf_op jit(solution)/shard_map/reduce-window
  7.2 0.1 copy.16
  7.6 10.1 %scatter_custom_fusion.1 = bf16[1280,2048]{1,0:T(8,128)(2,1)} fusion(s32[1024]{0:T(1024)S(1)} %bitcast.70, bf16[]{:T(256)} %constant.6.clone.1, bf16[128,2048]{1,0:T(8,128)(2,1)} %param.7), kind=kCustom, calls=%fused_computation.8 | custom fusion | bytes 5767170 | tf_op jit(solution)/shard_map/scatter | solution.py:58
  17.7 6.7 %all-to-all-start.1 = ((bf16[16,80,2048]{2,1,0:T(8,128)(2,1)}), bf16[16,80,2048]{2,1,0:T(8,128)(2,1)}, u32[]{:S(2)}, u32[]{:S(2)}) async-start(bf16[16,80,2048]{2,1,0:T(8,128)(2,1)} %bitcast.66), calls=%async_computation.1 | async-start | bytes 10485760 | tf_op jit(solution)/shard_map/all_to_all | solution.py:68
  24.4 0.1 copy.18
  24.7 10.1 %scatter_custom_fusion = bf16[1280,2048]{1,0:T(8,128)(2,1)} fusion(s32[1024]{0:T(1024)S(1)} %bitcast.71, f32[128,2048]{1,0:T(8,128)S(1)} %convert_element_type.37, f32[1024]{0:T(1024)S(1)} %mul.62, bf16[]{:T(256)} %constant.6.clone.1), kind=kCustom, calls=%fused_computation.6 | custom fusion | flops 4194304 | bytes 6295554 | tf_op jit(solution)/shard_map/scatter | solution.py:64
  34.8 104.5 %all-to-all-done.1 = bf16[16,80,2048]{2,1,0:T(8,128)(2,1)} async-done(((bf16[16,80,2048]{2,1,0:T(8,128)(2,1)}), bf16[16,80,2048]{2,1,0:T(8,128)(2,1)}, u32[]{:S(2)}, u32[]{:S(2)}) %all-to-all-start.1) | async-done | bytes 5242912 | tf_op jit(solution)/shard_map/all_to_all | solution.py:68
  139.3 4.9 %all-to-all-start = ((bf16[16,80,2048]{2,1,0:T(8,128)(2,1)}), bf16[16,80,2048]{2,1,0:T(8,128)(2,1)}, u32[]{:S(2)}, u32[]{:S(2)}) async-start(bf16[16,80,2048]{2,1,0:T(8,128)(2,1)} %bitcast.65), calls=%async_computation | async-start | bytes 10485760 | tf_op jit(solution)/shard_map/all_to_all | solution.py:69
  144.3 6.8 %fusion.16 = f32[1280,384]{1,0:T(8,128)} fusion(bf16[1280,2048]{1,0:T(8,128)(2,1)} %bitcast.10, bf16[1,2048,384]{2,1,0:T(8,128)(2,1)S(1)} %copy-done), kind=kOutput, calls=%fused_computation.28 | convolution fusion | flops 2013265920 | bytes 8781824 | tf_op jit(solution)/shard_map/dot_general | solution.py:8
  151.0 6.6 %fusion.19 = f32[1280,384]{1,0:T(8,128)} fusion(bf16[1280,2048]{1,0:T(8,128)(2,1)} %bitcast.10, bf16[1,2048,384]{2,1,0:T(8,128)(2,1)S(1)} %copy-done.1), kind=kOutput, calls=%fused_computation.31 | convolution fusion | flops 2013265920 | bytes 8781824 | tf_op jit(solution)/shard_map/dot_general | solution.py:9
  157.7 101.5 %all-to-all-done = bf16[16,80,2048]{2,1,0:T(8,128)(2,1)} async-done(((bf16[16,80,2048]{2,1,0:T(8,128)(2,1)}), bf16[16,80,2048]{2,1,0:T(8,128)(2,1)}, u32[]{:S(2)}, u32[]{:S(2)}) %all-to-all-start) | async-done | bytes 5242912 | tf_op jit(solution)/shard_map/all_to_all | solution.py:69
  259.2 7.5 %multiply_convert_fusion.1 = (bf16[1280,384]{1,0:T(8,128)(2,1)S(1)}, bf16[1280,384]{1,0:T(8,128)(2,1)S(1)}) fusion(f32[1280,384]{1,0:T(8,128)} %fusion.16, f32[1280,384]{1,0:T(8,128)} %fusion.19, bf16[1280,2048]{1,0:T(8,128)(2,1)} %bitcast.6, bf16[1,384,2048]{2,1,0:T(8,128)(2,1)} %param.13), kind=kOutput, calls=%fused_computation.22 | convolution fusion | flops 2019655680 | bytes 12713984 | tf_op jit(solution)/shard_map/dot_general | solution.py:13
  266.7 2.9 fusion.14
  269.7 4.7 %add_convert_fusion = bf16[1280,2048]{1,0:T(8,128)(2,1)} fusion(f32[1280,2048]{1,0:T(8,128)S(1)} %fusion.14, bf16[1280,384]{1,0:T(8,128)(2,1)S(1)} %get-tuple-element.4, bf16[1,2048,384]{2,1,0:T(8,128)(2,1)S(1)} %copy-done.1), kind=kOutput, calls=%fused_computation.3 | convolution fusion | flops 2018508800 | bytes 18284544 | tf_op jit(solution)/shard_map/dot_general | solution.py:20
  274.4 5.3 %all-to-all-start.2 = ((bf16[16,80,2048]{2,1,0:T(8,128)(2,1)}), bf16[16,80,2048]{2,1,0:T(8,128)(2,1)}, u32[]{:S(2)}, u32[]{:S(2)}) async-start(bf16[16,80,2048]{2,1,0:T(8,128)(2,1)} %bitcast.67), calls=%async_computation.2 | async-start | bytes 10485760 | tf_op jit(solution)/shard_map/all_to_all | solution.py:76
  279.7 6.6 %fusion.10 = bf16[1,2048,384]{2,1,0:T(8,128)(2,1)} fusion(bf16[1280,2048]{1,0:T(8,128)(2,1)} %bitcast.10, bf16[1280,384]{1,0:T(8,128)(2,1)S(1)} %copy-done.5), kind=kOutput, calls=%fused_computation.18 | convolution fusion | flops 2014052352 | bytes 7798784 | tf_op jit(solution)/shard_map/dot_general | solution.py:84
  286.4 6.7 %fusion.9 = bf16[1,2048,384]{2,1,0:T(8,128)(2,1)} fusion(bf16[1280,2048]{1,0:T(8,128)(2,1)} %bitcast.10, bf16[1280,384]{1,0:T(8,128)(2,1)S(1)} %copy-done.3), kind=kOutput, calls=%fused_computation.17 | convolution fusion | flops 2014052352 | bytes 7798784 | tf_op jit(solution)/shard_map/dot_general | solution.py:83
  293.1 6.0 %fusion.11 = bf16[1,384,2048]{2,1,0:T(8,128)(2,1)} fusion(bf16[1280,2048]{1,0:T(8,128)(2,1)} %bitcast.6, f32[1280,384]{1,0:T(8,128)S(1)} %copy-done.9, f32[1280,384]{1,0:T(8,128)S(1)} %copy-done.8), kind=kOutput, calls=%fused_computation.19 | convolution fusion | flops 2017001472 | bytes 10747904 | tf_op jit(solution)/shard_map/dot_general | solution.py:85
  299.1 95.5 %all-to-all-done.2 = bf16[16,80,2048]{2,1,0:T(8,128)(2,1)} async-done(((bf16[16,80,2048]{2,1,0:T(8,128)(2,1)}), bf16[16,80,2048]{2,1,0:T(8,128)(2,1)}, u32[]{:S(2)}, u32[]{:S(2)}) %all-to-all-start.2) | async-done | bytes 5242912 | tf_op jit(solution)/shard_map/all_to_all | solution.py:76
  394.6 12.0 %gather_fusion = bf16[1024,2048]{1,0:T(8,128)(2,1)} fusion(bf16[1280,2048]{1,0:T(8,128)(2,1)} %bitcast.14, s32[1024]{0:T(1024)S(1)} %broadcast_clamp_fusion), kind=kCustom, calls=%fused_computation | custom fusion | bytes 8392704 | tf_op jit(solution)/shard_map/gather | solution.py:86
  406.6 5.9 %bitcast_reduce_fusion = bf16[128,2048]{1,0:T(8,128)(2,1)} fusion(bf16[1024,2048]{1,0:T(8,128)(2,1)} %gather_fusion), kind=kLoop, calls=%fused_computation.7 | loop fusion | flops 1835008 | bytes 4718592 | tf_op jit(solution)/shard_map/reduce_sum | solution.py:87
  (35 shorter events, 0.8 us)
Async XLA Ops:
  0.6 143.6 %copy-start = (bf16[1,2048,384]{2,1,0:T(8,128)(2,1)S(1)}, bf16[1,2048,384]{2,1,0:T(8,128)(2,1)}, u32[]{:S(2)}) copy-start(bf16[1,2048,384]{2,1,0:T(8,128)(2,1)} %param.11) | copy-start | bytes 4718596
  17.7 6.7 %copy-start.7 = (f32[128,8]{0,1:T(8,128)S(1)}, f32[128,8]{0,1:T(8,128)}, u32[]{:S(2)}) copy-start(f32[128,8]{0,1:T(8,128)} %param.9) | copy-start | bytes 12292
  17.7 6.9 %copy-start.6 = (bf16[128,2048]{1,0:T(8,128)(2,1)S(1)}, bf16[128,2048]{1,0:T(8,128)(2,1)}, u32[]{:S(2)}) copy-start(bf16[128,2048]{1,0:T(8,128)(2,1)} %param.8) | copy-start | bytes 1572868
  17.7 121.6 %all-to-all-start.1 = ((bf16[16,80,2048]{2,1,0:T(8,128)(2,1)}), bf16[16,80,2048]{2,1,0:T(8,128)(2,1)}, u32[]{:S(2)}, u32[]{:S(2)}) async-start(bf16[16,80,2048]{2,1,0:T(8,128)(2,1)} %bitcast.66), calls=%async_computation.1 | async-start | bytes 10485760 | tf_op jit(solution)/shard_map/all_to_all | solution.py:68
  139.3 119.8 %all-to-all-start = ((bf16[16,80,2048]{2,1,0:T(8,128)(2,1)}), bf16[16,80,2048]{2,1,0:T(8,128)(2,1)}, u32[]{:S(2)}, u32[]{:S(2)}) async-start(bf16[16,80,2048]{2,1,0:T(8,128)(2,1)} %bitcast.65), calls=%async_computation | async-start | bytes 10485760 | tf_op jit(solution)/shard_map/all_to_all | solution.py:69
  144.2 6.8 %copy-start.1 = (bf16[1,2048,384]{2,1,0:T(8,128)(2,1)S(1)}, bf16[1,2048,384]{2,1,0:T(8,128)(2,1)}, u32[]{:S(2)}) copy-start(bf16[1,2048,384]{2,1,0:T(8,128)(2,1)} %param.12) | copy-start | bytes 4718596
  266.7 3.0 copy-start.2
  266.7 3.0 copy-start.4
  274.4 5.3 %copy-start.5 = (bf16[1280,384]{1,0:T(8,128)(2,1)S(1)}, bf16[1280,384]{1,0:T(8,128)(2,1)}, u32[]{:S(2)}) copy-start(bf16[1280,384]{1,0:T(8,128)(2,1)} %copy-done.4) | copy-start | bytes 2949124
  274.4 120.2 %all-to-all-start.2 = ((bf16[16,80,2048]{2,1,0:T(8,128)(2,1)}), bf16[16,80,2048]{2,1,0:T(8,128)(2,1)}, u32[]{:S(2)}, u32[]{:S(2)}) async-start(bf16[16,80,2048]{2,1,0:T(8,128)(2,1)} %bitcast.67), calls=%async_computation.2 | async-start | bytes 10485760 | tf_op jit(solution)/shard_map/all_to_all | solution.py:76
  279.7 6.7 %copy-start.3 = (bf16[1280,384]{1,0:T(8,128)(2,1)S(1)}, bf16[1280,384]{1,0:T(8,128)(2,1)}, u32[]{:S(2)}) copy-start(bf16[1280,384]{1,0:T(8,128)(2,1)} %copy-done.2) | copy-start | bytes 2949124
  286.4 6.7 %copy-start.8 = (f32[1280,384]{1,0:T(8,128)S(1)}, f32[1280,384]{1,0:T(8,128)}, u32[]{:S(2)}) copy-start(f32[1280,384]{1,0:T(8,128)} %fusion.16) | copy-start | bytes 5898244
  286.4 6.7 %copy-start.9 = (f32[1280,384]{1,0:T(8,128)S(1)}, f32[1280,384]{1,0:T(8,128)}, u32[]{:S(2)}) copy-start(f32[1280,384]{1,0:T(8,128)} %fusion.19) | copy-start | bytes 5898244
where the time goes:
time: 413 us; the launch traced here: 412 us
  waiting for transfers between devices  302 us (73%)
  matrix products  47.9 us (12%)
  local copies, waits for them, and re-layouts  23.7 us (6%)
  other arithmetic  21.6 us (5%)
  starting transfers between devices  16.9 us (4%)
    all_to_all x1, waiting for transfers between devices, local(): lax.all_to_all(send_inputs, 'expert', split_axis=0, concat_axis=0, tiled=...  105 us
    all_to_all x1, waiting for transfers between devices, local(): lax.all_to_all(send_grads, 'expert', split_axis=0, concat_axis=0, tiled=T...  102 us
    all_to_all x1, waiting for transfers between devices, local(): lax.all_to_all(row_grad.reshape(experts, capacity, width), 'expert', spli...  95.5 us
    gather x1, local copies, waits for them, and re-layouts, local(): returned.reshape(row_total, width)[places]  12 us
    scatter x1, other arithmetic, local(): send_grads = jnp.zeros((row_total, width), jnp.bfloat16).at[places].set(r...  10.1 us
    scatter x1, local copies, waits for them, and re-layouts, local(): send_inputs = jnp.zeros((row_total, width), jnp.bfloat16).at[places].set(...  10.1 us
  transfers between devices with their start and end apart: 3, of which 3 were waited for; matrix products, arithmetic and copies ran while one was open for 10% of the time, Pallas kernels for 0%

commit v1 on v0

--- a/solution.py
+++ b/solution.py
@@ -64,9 +64,27 @@
         .set(route_grads)
         .reshape(experts, capacity, width)
     )
+
+    def place_panels(block_here):
+        e_next, mid_arr = (lax.axis_size("expert"), lax.axis_index("expert"))
+        placed = block_here.shape[0] // e_next
+        item_now = list(block_here.shape)
+        item_now[0] = placed
+        right_arr = item_now[0]
+        item_now[0] = right_arr * e_next
+        state_now = jnp.zeros(item_now, block_here.dtype)
+        for w in range(e_next):
+            a_next = lax.dynamic_slice_in_dim(block_here, (mid_arr ^ w) * placed, placed, axis=0)
+            if w:
+                a_next = lax.ppermute(a_next, "expert", tuple(((q, q ^ w) for q in range(e_next))))
+            state_now = lax.dynamic_update_slice_in_dim(
+                state_now, a_next, (mid_arr ^ w) * right_arr, axis=0
+            )
+        return state_now
+
     got_inputs, got_grads = (
         lax.all_to_all(send_inputs, "expert", split_axis=0, concat_axis=0, tiled=True),
-        lax.all_to_all(send_grads, "expert", split_axis=0, concat_axis=0, tiled=True),
+        place_panels(send_grads),
     )
     flat_in = got_inputs.reshape(row_total, width)
     flat_grad = got_grads.reshape(row_total, width)

time: 413 us -> 433 us (1.048); the launches traced: 412 us -> 424 us
  waiting for transfers between devices: 302 us -> 274 us
  starting transfers between devices: 16.9 us -> 42.3 us
  local copies, waits for them, and re-layouts: 23.7 us -> 41.3 us
    ppermute x0 -> x15, waiting for transfers between devices: none -> 178 us  [place_panels(): lax.ppermute(a_next, 'expert', tuple(((q, q ^ w) for q in range(e_next))))]
    all_to_all x1, waiting for transfers between devices: 105 us -> 0.01 us  [local(): lax.all_to_all(send_inputs, 'expert', split_axis=0, concat_axis=0, tiled=...]
    all_to_all x1 -> x0, waiting for transfers between devices: 102 us -> none  [local(): lax.all_to_all(send_grads, 'expert', split_axis=0, concat_axis=0, tiled=T...]
    ppermute x0 -> x15, starting transfers between devices: none -> 29.7 us  [place_panels(): lax.ppermute(a_next, 'expert', tuple(((q, q ^ w) for q in range(e_next))))]
    dynamic_update_slice x0 -> x15, local copies, waits for them, and re-layouts: none -> 11.3 us  [place_panels(): lax.dynamic_update_slice_in_dim(state_now, a_next, (mid_arr ^ w) * right_...]
    all_to_all x1 -> x0, starting transfers between devices: 4.91 us -> none  [local(): lax.all_to_all(send_grads, 'expert', split_axis=0, concat_axis=0, tiled=T...]
  transfers between devices with their start and end apart: 3 -> 17, of which waited for: 3 -> 12; matrix products, arithmetic and copies ran while one was open for 10% -> 11% of each run, Pallas kernels for 0% -> 0%
where the time goes in v1:
time: 433 us; the launch traced here: 424 us
  waiting for transfers between devices  274 us (63%)
  matrix products  44.2 us (10%)
  starting transfers between devices  42.3 us (10%)
  local copies, waits for them, and re-layouts  41.3 us (10%)
  other arithmetic  22 us (5%)
    ppermute x15, waiting for transfers between devices, place_panels(): lax.ppermute(a_next, 'expert', tuple(((q, q ^ w) for q in range(e_next))))  178 us
    all_to_all x1, waiting for transfers between devices, local(): lax.all_to_all(row_grad.reshape(experts, capacity, width), 'expert', spli...  95.5 us
    ppermute x15, starting transfers between devices, place_panels(): lax.ppermute(a_next, 'expert', tuple(((q, q ^ w) for q in range(e_next))))  29.7 us
    gather x1, local copies, waits for them, and re-layouts, local(): returned.reshape(row_total, width)[places]  12.3 us
    dynamic_update_slice x15, local copies, waits for them, and re-layouts, place_panels(): lax.dynamic_update_slice_in_dim(state_now, a_next, (mid_arr ^ w) * right_...  11.3 us
    scatter x1, other arithmetic, local(): send_grads = jnp.zeros((row_total, width), jnp.bfloat16).at[places].set(r...  10.5 us
    scatter x1, local copies, waits for them, and re-layouts, local(): send_inputs = jnp.zeros((row_total, width), jnp.bfloat16).at[places].set(...  10.1 us
  transfers between devices with their start and end apart: 17, of which 12 were waited for; matrix products, arithmetic and copies ran while one was open for 11% of the time, Pallas kernels for 0%

profile of v1, /device:TPU:13, one launch (start us, length us, event | category | flops | bytes accessed | tf_op | source)
XLA Modules:
  0.0 424.4 jit_solution(1696626243027350214)
XLA Ops:
  7.6 10.1 %scatter_custom_fusion.1 = bf16[1280,2048]{1,0:T(8,128)(2,1)} fusion(s32[1024]{0:T(1024)S(1)} %bitcast.70, bf16[]{:T(256)} %constant.23.clone.1, bf16[128,2048]{1,0:T(8,128)(2,1)} %param.7), kind=kCustom, calls=%fused_computation.8 | custom fusion | bytes 5767170 | tf_op jit(solution)/shard_map/scatter | solution.py:58
  17.7 6.7 %all-to-all-start = ((bf16[16,80,2048]{2,1,0:T(8,128)(2,1)}), bf16[16,80,2048]{2,1,0:T(8,128)(2,1)}, u32[]{:S(2)}, u32[]{:S(2)}) async-start(bf16[16,80,2048]{2,1,0:T(8,128)(2,1)} %bitcast.65), calls=%async_computation | async-start | bytes 10485760 | tf_op jit(solution)/shard_map/all_to_all | solution.py:86
  24.8 10.5 %scatter_custom_fusion = bf16[1280,2048]{1,0:T(8,128)(2,1)} fusion(s32[1024]{0:T(1024)S(1)} %bitcast.71, f32[128,2048]{1,0:T(8,128)S(1)} %convert_element_type.37, f32[1024]{0:T(1024)S(1)} %mul.62, bf16[]{:T(256)} %constant.23.clone.1), kind=kCustom, calls=%fused_computation.6 | custom fusion | flops 4194304 | bytes 6295554 | tf_op jit(solution)/shard_map/scatter | solution.py:64
  48.1 12.7 %collective-permute-done.1 = bf16[1,80,2048]{2,1,0:T(8,128)(2,1)S(1)} collective-permute-done((bf16[1,80,2048]{2,1,0:T(8,128)(2,1)S(1)}, bf16[1,80,2048]{2,1,0:T(8,128)(2,1)S(1)}, u32[]{:S(2)}, u32[]{:S(2)}) %collective-permute-start.1) | collective-permute-done | bytes 327712 | tf_op jit(solution)/shard_map/ppermute | solution.py:79
  62.0 6.0 %collective-permute-done.2 = bf16[1,80,2048]{2,1,0:T(8,128)(2,1)S(1)} collective-permute-done((bf16[1,80,2048]{2,1,0:T(8,128)(2,1)S(1)}, bf16[1,80,2048]{2,1,0:T(8,128)(2,1)S(1)}, u32[]{:S(2)}, u32[]{:S(2)}) %collective-permute-start.2) | collective-permute-done | bytes 327712 | tf_op jit(solution)/shard_map/ppermute | solution.py:79
  68.0 8.8 %collective-permute-start.4 = (bf16[1,80,2048]{2,1,0:T(8,128)(2,1)S(1)}, bf16[1,80,2048]{2,1,0:T(8,128)(2,1)S(1)}, u32[]{:S(2)}, u32[]{:S(2)}) collective-permute-start(bf16[1,80,2048]{2,1,0:T(8,128)(2,1)S(1)} %get-tuple-element.14), channel_id=1, source_target_pairs={{0,5},{1,4},{2,7},{3,6},{4,1},{5,0},{6,3},{7,2},{8,13},{9,12},{10,... | collective-permute-start | bytes 983048 | tf_op jit(solution)/shard_map/ppermute | solution.py:79
  77.6 61.7 %collective-permute-done.3 = bf16[1,80,2048]{2,1,0:T(8,128)(2,1)S(1)} collective-permute-done((bf16[1,80,2048]{2,1,0:T(8,128)(2,1)S(1)}, bf16[1,80,2048]{2,1,0:T(8,128)(2,1)S(1)}, u32[]{:S(2)}, u32[]{:S(2)}) %collective-permute-start.3) | collective-permute-done | bytes 327712 | tf_op jit(solution)/shard_map/ppermute | solution.py:79
  140.0 7.2 %collective-permute-done.4 = bf16[1,80,2048]{2,1,0:T(8,128)(2,1)S(1)} collective-permute-done((bf16[1,80,2048]{2,1,0:T(8,128)(2,1)S(1)}, bf16[1,80,2048]{2,1,0:T(8,128)(2,1)S(1)}, u32[]{:S(2)}, u32[]{:S(2)}) %collective-permute-start.4) | collective-permute-done | bytes 327712 | tf_op jit(solution)/shard_map/ppermute | solution.py:79
  152.5 9.6 %collective-permute-start.7 = (bf16[1,80,2048]{2,1,0:T(8,128)(2,1)S(1)}, bf16[1,80,2048]{2,1,0:T(8,128)(2,1)S(1)}, u32[]{:S(2)}, u32[]{:S(2)}) collective-permute-start(bf16[1,80,2048]{2,1,0:T(8,128)(2,1)S(1)} %get-tuple-element.11), channel_id=1, source_target_pairs={{0,8},{1,9},{2,10},{3,11},{4,12},{5,13},{6,14},{7,15},{8,0},{9,1},... | collective-permute-start | bytes 983048 | tf_op jit(solution)/shard_map/ppermute | solution.py:79
  170.3 36.7 %collective-permute-done.7 = bf16[1,80,2048]{2,1,0:T(8,128)(2,1)S(1)} collective-permute-done((bf16[1,80,2048]{2,1,0:T(8,128)(2,1)S(1)}, bf16[1,80,2048]{2,1,0:T(8,128)(2,1)S(1)}, u32[]{:S(2)}, u32[]{:S(2)}) %collective-permute-start.7) | collective-permute-done | bytes 327712 | tf_op jit(solution)/shard_map/ppermute | solution.py:79
  207.8 13.3 %collective-permute-done.8 = bf16[1,80,2048]{2,1,0:T(8,128)(2,1)S(1)} collective-permute-done((bf16[1,80,2048]{2,1,0:T(8,128)(2,1)S(1)}, bf16[1,80,2048]{2,1,0:T(8,128)(2,1)S(1)}, u32[]{:S(2)}, u32[]{:S(2)}) %collective-permute-start.8) | collective-permute-done | bytes 327712 | tf_op jit(solution)/shard_map/ppermute | solution.py:79
  221.8 13.3 %collective-permute-done.9 = bf16[1,80,2048]{2,1,0:T(8,128)(2,1)S(1)} collective-permute-done((bf16[1,80,2048]{2,1,0:T(8,128)(2,1)S(1)}, bf16[1,80,2048]{2,1,0:T(8,128)(2,1)S(1)}, u32[]{:S(2)}, u32[]{:S(2)}) %collective-permute-start.9) | collective-permute-done | bytes 327712 | tf_op jit(solution)/shard_map/ppermute | solution.py:79
  236.2 13.0 %collective-permute-done.10 = bf16[1,80,2048]{2,1,0:T(8,128)(2,1)S(1)} collective-permute-done((bf16[1,80,2048]{2,1,0:T(8,128)(2,1)S(1)}, bf16[1,80,2048]{2,1,0:T(8,128)(2,1)S(1)}, u32[]{:S(2)}, u32[]{:S(2)}) %collective-permute-start.10) | collective-permute-done | bytes 327712 | tf_op jit(solution)/shard_map/ppermute | solution.py:79
  249.9 7.3 %collective-permute-done.11 = bf16[1,80,2048]{2,1,0:T(8,128)(2,1)S(1)} collective-permute-done((bf16[1,80,2048]{2,1,0:T(8,128)(2,1)S(1)}, bf16[1,80,2048]{2,1,0:T(8,128)(2,1)S(1)}, u32[]{:S(2)}, u32[]{:S(2)}) %collective-permute-start.11) | collective-permute-done | bytes 327712 | tf_op jit(solution)/shard_map/ppermute | solution.py:79
  260.2 4.9 %fusion.16 = f32[1280,384]{1,0:T(8,128)S(1)} fusion(bf16[1280,2048]{1,0:T(8,128)(2,1)} %bitcast.10, bf16[1,2048,384]{2,1,0:T(8,128)(2,1)S(1)} %copy-done), kind=kOutput, calls=%fused_computation.28 | convolution fusion | flops 2013265920 | bytes 8781824 | tf_op jit(solution)/shard_map/dot_general | solution.py:8
  265.2 5.6 %fusion.19 = f32[1280,384]{1,0:T(8,128)S(1)} fusion(bf16[1280,2048]{1,0:T(8,128)(2,1)} %bitcast.10, bf16[1,2048,384]{2,1,0:T(8,128)(2,1)S(1)} %copy-done.3), kind=kOutput, calls=%fused_computation.31 | convolution fusion | flops 2013265920 | bytes 8781824 | tf_op jit(solution)/shard_map/dot_general | solution.py:9
  270.8 6.8 %multiply_convert_fusion.1 = (bf16[1280,384]{1,0:T(8,128)(2,1)S(1)}, bf16[1280,384]{1,0:T(8,128)(2,1)S(1)}) fusion(f32[1280,384]{1,0:T(8,128)S(1)} %fusion.16, f32[1280,384]{1,0:T(8,128)S(1)} %fusion.19, bf16[1280,2048]{1,0:T(8,128)(2,1)} %bitcast.6, bf16[1,384,2048]{2,1,0:T(8,128)(2,1)S(1)} %copy-done.6), kind=kOutput, calls=%fused_computation.22 | convolution fusion | flops 2019655680 | bytes 12713984 | tf_op jit(solution)/shard_map/dot_general | solution.py:13
  285.3 5.9 %all-to-all-start.1 = ((bf16[16,80,2048]{2,1,0:T(8,128)(2,1)}), bf16[16,80,2048]{2,1,0:T(8,128)(2,1)}, u32[]{:S(2)}, u32[]{:S(2)}) async-start(bf16[16,80,2048]{2,1,0:T(8,128)(2,1)} %bitcast.67), calls=%async_computation.1 | async-start | bytes 10485760 | tf_op jit(solution)/shard_map/all_to_all | solution.py:94
  291.2 6.6 %fusion.10 = bf16[1,2048,384]{2,1,0:T(8,128)(2,1)} fusion(bf16[1280,2048]{1,0:T(8,128)(2,1)} %bitcast.10, bf16[1280,384]{1,0:T(8,128)(2,1)S(1)} %get-tuple-element.20), kind=kOutput, calls=%fused_computation.18 | convolution fusion | flops 2014052352 | bytes 7798784 | tf_op jit(solution)/shard_map/dot_general | solution.py:102
  297.8 6.7 %fusion.9 = bf16[1,2048,384]{2,1,0:T(8,128)(2,1)} fusion(bf16[1280,2048]{1,0:T(8,128)(2,1)} %bitcast.10, bf16[1280,384]{1,0:T(8,128)(2,1)S(1)} %get-tuple-element.21), kind=kOutput, calls=%fused_computation.17 | convolution fusion | flops 2014052352 | bytes 7798784 | tf_op jit(solution)/shard_map/dot_general | solution.py:101
  304.5 6.0 %fusion.11 = bf16[1,384,2048]{2,1,0:T(8,128)(2,1)} fusion(bf16[1280,2048]{1,0:T(8,128)(2,1)} %bitcast.6, f32[1280,384]{1,0:T(8,128)S(1)} %copy-done.10, f32[1280,384]{1,0:T(8,128)S(1)} %copy-done.8), kind=kOutput, calls=%fused_computation.19 | convolution fusion | flops 2017001472 | bytes 10747904 | tf_op jit(solution)/shard_map/dot_general | solution.py:103
  310.5 95.5 %all-to-all-done.1 = bf16[16,80,2048]{2,1,0:T(8,128)(2,1)} async-done(((bf16[16,80,2048]{2,1,0:T(8,128)(2,1)}), bf16[16,80,2048]{2,1,0:T(8,128)(2,1)}, u32[]{:S(2)}, u32[]{:S(2)}) %all-to-all-start.1) | async-done | bytes 5242912 | tf_op jit(solution)/shard_map/all_to_all | solution.py:94
  406.0 12.3 %gather_fusion = bf16[1024,2048]{1,0:T(8,128)(2,1)} fusion(bf16[1280,2048]{1,0:T(8,128)(2,1)} %bitcast.14, s32[1024]{0:T(1024)S(1)} %broadcast_clamp_fusion), kind=kCustom, calls=%fused_computation | custom fusion | bytes 8392704 | tf_op jit(solution)/shard_map/gather | solution.py:104
  418.3 5.9 %bitcast_reduce_fusion = bf16[128,2048]{1,0:T(8,128)(2,1)} fusion(bf16[1024,2048]{1,0:T(8,128)(2,1)} %gather_fusion), kind=kLoop, calls=%fused_computation.7 | loop fusion | flops 1835008 | bytes 4718592 | tf_op jit(solution)/shard_map/reduce_sum | solution.py:105
  (82 shorter events, 50.2 us)
Async XLA Ops:
  0.6 259.6 %copy-start = (bf16[1,2048,384]{2,1,0:T(8,128)(2,1)S(1)}, bf16[1,2048,384]{2,1,0:T(8,128)(2,1)}, u32[]{:S(2)}) copy-start(bf16[1,2048,384]{2,1,0:T(8,128)(2,1)} %param.11) | copy-start | bytes 4718596
  17.7 6.7 %copy-start.5 = (f32[128,8]{0,1:T(8,128)S(1)}, f32[128,8]{0,1:T(8,128)}, u32[]{:S(2)}) copy-start(f32[128,8]{0,1:T(8,128)} %param.9) | copy-start | bytes 12292
  17.7 6.9 %copy-start.4 = (bf16[128,2048]{1,0:T(8,128)(2,1)S(1)}, bf16[128,2048]{1,0:T(8,128)(2,1)}, u32[]{:S(2)}) copy-start(bf16[128,2048]{1,0:T(8,128)(2,1)} %param.8) | copy-start | bytes 1572868
  17.7 242.5 %all-to-all-start = ((bf16[16,80,2048]{2,1,0:T(8,128)(2,1)}), bf16[16,80,2048]{2,1,0:T(8,128)(2,1)}, u32[]{:S(2)}, u32[]{:S(2)}) async-start(bf16[16,80,2048]{2,1,0:T(8,128)(2,1)} %bitcast.65), calls=%async_computation | async-start | bytes 10485760 | tf_op jit(solution)/shard_map/all_to_all | solution.py:86
  41.3 4.8 %collective-permute-start = (bf16[1,80,2048]{2,1,0:T(8,128)(2,1)S(1)}, bf16[1,80,2048]{2,1,0:T(8,128)(2,1)S(1)}, u32[]{:S(2)}, u32[]{:S(2)}) collective-permute-start(bf16[1,80,2048]{2,1,0:T(8,128)(2,1)S(1)} %get-tuple-element.18), channel_id=1, source_target_pairs={{0,1},{1,0},{2,3},{3,2},{4,5},{5,4},{6,7},{7,6},{8,9},{9,8},{10,11... | collective-permute-start | bytes 983048 | tf_op jit(solution)/shard_map/ppermute | solution.py:79
  41.7 19.1 %collective-permute-start.1 = (bf16[1,80,2048]{2,1,0:T(8,128)(2,1)S(1)}, bf16[1,80,2048]{2,1,0:T(8,128)(2,1)S(1)}, u32[]{:S(2)}, u32[]{:S(2)}) collective-permute-start(bf16[1,80,2048]{2,1,0:T(8,128)(2,1)S(1)} %get-tuple-element.17), channel_id=1, source_target_pairs={{0,2},{1,3},{2,0},{3,1},{4,6},{5,7},{6,4},{7,5},{8,10},{9,11},{10,... | collective-permute-start | bytes 983048 | tf_op jit(solution)/shard_map/ppermute | solution.py:79
  41.9 217.5 %collective-permute-start.14 = (bf16[1,80,2048]{2,1,0:T(8,128)(2,1)S(1)}, bf16[1,80,2048]{2,1,0:T(8,128)(2,1)S(1)}, u32[]{:S(2)}, u32[]{:S(2)}) collective-permute-start(bf16[1,80,2048]{2,1,0:T(8,128)(2,1)S(1)} %get-tuple-element.4), channel_id=1, source_target_pairs={{0,15},{1,14},{2,13},{3,12},{4,11},{5,10},{6,9},{7,8},{8,7},{9,6},... | collective-permute-start | bytes 983048 | tf_op jit(solution)/shard_map/ppermute | solution.py:79
  44.4 214.4 %collective-permute-start.13 = (bf16[1,80,2048]{2,1,0:T(8,128)(2,1)S(1)}, bf16[1,80,2048]{2,1,0:T(8,128)(2,1)S(1)}, u32[]{:S(2)}, u32[]{:S(2)}) collective-permute-start(bf16[1,80,2048]{2,1,0:T(8,128)(2,1)S(1)} %get-tuple-element.5), channel_id=1, source_target_pairs={{0,14},{1,15},{2,12},{3,13},{4,10},{5,11},{6,8},{7,9},{8,6},{9,7},... | collective-permute-start | bytes 983048 | tf_op jit(solution)/shard_map/ppermute | solution.py:79
  44.6 213.4 %collective-permute-start.12 = (bf16[1,80,2048]{2,1,0:T(8,128)(2,1)S(1)}, bf16[1,80,2048]{2,1,0:T(8,128)(2,1)S(1)}, u32[]{:S(2)}, u32[]{:S(2)}) collective-permute-start(bf16[1,80,2048]{2,1,0:T(8,128)(2,1)S(1)} %get-tuple-element.6), channel_id=1, source_target_pairs={{0,13},{1,12},{2,15},{3,14},{4,9},{5,8},{6,11},{7,10},{8,5},{9,4},... | collective-permute-start | bytes 983048 | tf_op jit(solution)/shard_map/ppermute | solution.py:79
  46.1 21.9 %collective-permute-start.2 = (bf16[1,80,2048]{2,1,0:T(8,128)(2,1)S(1)}, bf16[1,80,2048]{2,1,0:T(8,128)(2,1)S(1)}, u32[]{:S(2)}, u32[]{:S(2)}) collective-permute-start(bf16[1,80,2048]{2,1,0:T(8,128)(2,1)S(1)} %get-tuple-element.16), channel_id=1, source_target_pairs={{0,3},{1,2},{2,1},{3,0},{4,7},{5,6},{6,5},{7,4},{8,11},{9,10},{10,... | collective-permute-start | bytes 983048 | tf_op jit(solution)/shard_map/ppermute | solution.py:79
  60.8 78.5 %collective-permute-start.3 = (bf16[1,80,2048]{2,1,0:T(8,128)(2,1)S(1)}, bf16[1,80,2048]{2,1,0:T(8,128)(2,1)S(1)}, u32[]{:S(2)}, u32[]{:S(2)}) collective-permute-start(bf16[1,80,2048]{2,1,0:T(8,128)(2,1)S(1)} %get-tuple-element.15), channel_id=1, source_target_pairs={{0,4},{1,5},{2,6},{3,7},{4,0},{5,1},{6,2},{7,3},{8,12},{9,13},{10,... | collective-permute-start | bytes 983048 | tf_op jit(solution)/shard_map/ppermute | solution.py:79
  68.0 79.2 %collective-permute-start.4 = (bf16[1,80,2048]{2,1,0:T(8,128)(2,1)S(1)}, bf16[1,80,2048]{2,1,0:T(8,128)(2,1)S(1)}, u32[]{:S(2)}, u32[]{:S(2)}) collective-permute-start(bf16[1,80,2048]{2,1,0:T(8,128)(2,1)S(1)} %get-tuple-element.14), channel_id=1, source_target_pairs={{0,5},{1,4},{2,7},{3,6},{4,1},{5,0},{6,3},{7,2},{8,13},{9,12},{10,... | collective-permute-start | bytes 983048 | tf_op jit(solution)/shard_map/ppermute | solution.py:79
  139.3 13.3 %collective-permute-start.5 = (bf16[1,80,2048]{2,1,0:T(8,128)(2,1)S(1)}, bf16[1,80,2048]{2,1,0:T(8,128)(2,1)S(1)}, u32[]{:S(2)}, u32[]{:S(2)}) collective-permute-start(bf16[1,80,2048]{2,1,0:T(8,128)(2,1)S(1)} %get-tuple-element.13), channel_id=1, source_target_pairs={{0,6},{1,7},{2,4},{3,5},{4,2},{5,3},{6,0},{7,1},{8,14},{9,15},{10,... | collective-permute-start | bytes 983048 | tf_op jit(solution)/shard_map/ppermute | solution.py:79
  147.2 17.8 %collective-permute-start.6 = (bf16[1,80,2048]{2,1,0:T(8,128)(2,1)S(1)}, bf16[1,80,2048]{2,1,0:T(8,128)(2,1)S(1)}, u32[]{:S(2)}, u32[]{:S(2)}) collective-permute-start(bf16[1,80,2048]{2,1,0:T(8,128)(2,1)S(1)} %get-tuple-element.12), channel_id=1, source_target_pairs={{0,7},{1,6},{2,5},{3,4},{4,3},{5,2},{6,1},{7,0},{8,15},{9,14},{10,... | collective-permute-start | bytes 983048 | tf_op jit(solution)/shard_map/ppermute | solution.py:79
  152.5 54.5 %collective-permute-start.7 = (bf16[1,80,2048]{2,1,0:T(8,128)(2,1)S(1)}, bf16[1,80,2048]{2,1,0:T(8,128)(2,1)S(1)}, u32[]{:S(2)}, u32[]{:S(2)}) collective-permute-start(bf16[1,80,2048]{2,1,0:T(8,128)(2,1)S(1)} %get-tuple-element.11), channel_id=1, source_target_pairs={{0,8},{1,9},{2,10},{3,11},{4,12},{5,13},{6,14},{7,15},{8,0},{9,1},... | collective-permute-start | bytes 983048 | tf_op jit(solution)/shard_map/ppermute | solution.py:79
  165.0 56.0 %collective-permute-start.8 = (bf16[1,80,2048]{2,1,0:T(8,128)(2,1)S(1)}, bf16[1,80,2048]{2,1,0:T(8,128)(2,1)S(1)}, u32[]{:S(2)}, u32[]{:S(2)}) collective-permute-start(bf16[1,80,2048]{2,1,0:T(8,128)(2,1)S(1)} %get-tuple-element.10), channel_id=1, source_target_pairs={{0,9},{1,8},{2,11},{3,10},{4,13},{5,12},{6,15},{7,14},{8,1},{9,0},... | collective-permute-start | bytes 983048 | tf_op jit(solution)/shard_map/ppermute | solution.py:79
  207.0 28.1 %collective-permute-start.9 = (bf16[1,80,2048]{2,1,0:T(8,128)(2,1)S(1)}, bf16[1,80,2048]{2,1,0:T(8,128)(2,1)S(1)}, u32[]{:S(2)}, u32[]{:S(2)}) collective-permute-start(bf16[1,80,2048]{2,1,0:T(8,128)(2,1)S(1)} %get-tuple-element.9), channel_id=1, source_target_pairs={{0,10},{1,11},{2,8},{3,9},{4,14},{5,15},{6,12},{7,13},{8,2},{9,3},... | collective-permute-start | bytes 983048 | tf_op jit(solution)/shard_map/ppermute | solution.py:79
  221.1 28.1 %collective-permute-start.10 = (bf16[1,80,2048]{2,1,0:T(8,128)(2,1)S(1)}, bf16[1,80,2048]{2,1,0:T(8,128)(2,1)S(1)}, u32[]{:S(2)}, u32[]{:S(2)}) collective-permute-start(bf16[1,80,2048]{2,1,0:T(8,128)(2,1)S(1)} %get-tuple-element.8), channel_id=1, source_target_pairs={{0,11},{1,10},{2,9},{3,8},{4,15},{5,14},{6,13},{7,12},{8,3},{9,2},... | collective-permute-start | bytes 983048 | tf_op jit(solution)/shard_map/ppermute | solution.py:79
  235.1 22.1 %collective-permute-start.11 = (bf16[1,80,2048]{2,1,0:T(8,128)(2,1)S(1)}, bf16[1,80,2048]{2,1,0:T(8,128)(2,1)S(1)}, u32[]{:S(2)}, u32[]{:S(2)}) collective-permute-start(bf16[1,80,2048]{2,1,0:T(8,128)(2,1)S(1)} %get-tuple-element.7), channel_id=1, source_target_pairs={{0,12},{1,13},{2,14},{3,15},{4,8},{5,9},{6,10},{7,11},{8,4},{9,5},... | collective-permute-start | bytes 983048 | tf_op jit(solution)/shard_map/ppermute | solution.py:79
  270.8 6.8 %copy-start.9 = (f32[1280,384]{1,0:T(8,128)}, f32[1280,384]{1,0:T(8,128)S(1)}, u32[]{:S(2)}) copy-start(f32[1280,384]{1,0:T(8,128)S(1)} %fusion.19) | copy-start | bytes 5898244
  285.3 120.7 %all-to-all-start.1 = ((bf16[16,80,2048]{2,1,0:T(8,128)(2,1)}), bf16[16,80,2048]{2,1,0:T(8,128)(2,1)}, u32[]{:S(2)}, u32[]{:S(2)}) async-start(bf16[16,80,2048]{2,1,0:T(8,128)(2,1)} %bitcast.67), calls=%async_computation.1 | async-start | bytes 10485760 | tf_op jit(solution)/shard_map/all_to_all | solution.py:94
  297.8 6.7 %copy-start.8 = (f32[1280,384]{1,0:T(8,128)S(1)}, f32[1280,384]{1,0:T(8,128)}, u32[]{:S(2)}) copy-start(f32[1280,384]{1,0:T(8,128)} %copy-done.7) | copy-start | bytes 5898244
  297.8 6.7 %copy-start.10 = (f32[1280,384]{1,0:T(8,128)S(1)}, f32[1280,384]{1,0:T(8,128)}, u32[]{:S(2)}) copy-start(f32[1280,384]{1,0:T(8,128)} %copy-done.9) | copy-start | bytes 5898244
  406.0 18.2 %copy-start.1 = (bf16[1,2048,384]{2,1,0:T(8,128)(2,1)S(1)}, bf16[1,2048,384]{2,1,0:T(8,128)(2,1)}, u32[]{:S(2)}) copy-start(bf16[1,2048,384]{2,1,0:T(8,128)(2,1)} %param.11) | copy-start | bytes 4718596
  (4 other events, 20.5 us)
